TPU v7x, 32 devices: a whole 2x2x4 slice. The times are simulated.
32 devices in a mesh: gx: 4 (over y, x), gz: 8 (over z, core).
Axes of the slice: x: 2, y: 2, z: 4, core: 2. Of those that a mesh axis runs over, the one named last changes fastest.
Arguments:
- pop_ratio: float32 [19, 16, 64, 512], P(None, None, 'gz', 'gx'), may hold values from 0.6 to 1.4
- solid_blocks: int32 [4, 16, 128], P(None, 'gz', 'gx'), may hold values 0 or 1
- shift_whole: int32 [2], replicated, may hold values from 0 to 511
- shift_frac: int32 [2], replicated, may hold values from 0 to 4095
Outputs:
- populations: float32 [19, 16, 64, 512], P(None, None, 'gz', 'gx')
- accumulated: float32 [2, 16, 64, 512], P(None, None, 'gz', 'gx')
- profiles: float32 [2, 16, 64], P(None, None, 'gz')
Inputs may be any that keep to these rules, and one draw needn't show every extreme that they name: `shift_whole`: whole cells of the displacement, below 512.
All inputs are finite; a program needn't handle non-finite values. No bound on the sum of `solid_blocks` on one device may be relied on, other than what follows from the above.
Results may differ from a plain program's by a relative error of at most 0.00023.
Values sent between devices are 32-bit elements; how exact they have to be, the bound alone decides.
No kernel may reach another device: no remote copies, remote signals or barrier semaphores. Data moves between devices by JAX's collectives and lax.ppermute only.
A program may use at most 64 MiB of HBM per device.

v0:
```python
import jax
import jax.numpy as jnp
import numpy as np
from jax import lax
from jax.sharding import PartitionSpec as P

STEPS = 2
BLOCK = 4
velocity_list = [
    (0, 0, 0),
    (1, 0, 0),
    (-1, 0, 0),
    (0, 1, 0),
    (0, -1, 0),
    (0, 0, 1),
    (0, 0, -1),
    (1, 1, 0),
    (-1, -1, 0),
    (1, -1, 0),
    (-1, 1, 0),
    (1, 0, 1),
    (-1, 0, -1),
    (1, 0, -1),
    (-1, 0, 1),
    (0, 1, 1),
    (0, -1, -1),
    (0, 1, -1),
    (0, -1, 1),
]
velocities = np.array(velocity_list)
lattice_weights = np.array([1.0 / 3.0] + [1.0 / 18.0] * 6 + [1.0 / 36.0] * 12)
opposite = np.array(
    [velocity_list.index((-entry[0], -entry[1], -entry[2])) for entry in velocity_list]
)
rising = [index for index in range(19) if velocities[index, 1] == 1]
falling = [index for index in range(19) if velocities[index, 1] == -1]
wall_speed = 0.08
visc_rate = 1.25
fraction_unit = 4096.0
relax_rates = np.array(
    [
        0.0,
        1.19,
        1.4,
        0.0,
        1.2,
        0.0,
        1.2,
        0.0,
        1.2,
        1.25,
        1.4,
        1.25,
        1.4,
        1.25,
        1.25,
        1.25,
        1.98,
        1.98,
        1.98,
    ]
)


def extended(value, sides, width):
    for axis, dim in sides:
        count, length = (lax.axis_size(axis), value.shape[dim])
        up = [(i, (i + 1) % count) for i in range(count)]
        down = [(j, i) for i, j in up]
        last = lax.slice_in_dim(value, length - width, length, axis=dim)
        initial = lax.slice_in_dim(value, 0, width, axis=dim)
        before = lax.ppermute(last, axis, up)
        after = lax.ppermute(initial, axis, down)
        value = jnp.concatenate([before, value, after], axis=dim)
    return value


def moment_rows():
    vel_x = velocities[:, 0] * 1.0
    vel_y = velocities[:, 1] * 1.0
    vel_z = velocities[:, 2] * 1.0
    speed_sq = vel_x * vel_x + vel_y * vel_y + vel_z * vel_z
    rows = [
        np.ones(19),
        19 * speed_sq - 30,
        (21 * speed_sq * speed_sq - 53 * speed_sq + 24) / 2,
        vel_x,
        (5 * speed_sq - 9) * vel_x,
        vel_y,
        (5 * speed_sq - 9) * vel_y,
        vel_z,
        (5 * speed_sq - 9) * vel_z,
        3 * vel_x * vel_x - speed_sq,
        (3 * speed_sq - 5) * (3 * vel_x * vel_x - speed_sq),
        vel_y * vel_y - vel_z * vel_z,
        (3 * speed_sq - 5) * (vel_y * vel_y - vel_z * vel_z),
        vel_x * vel_y,
        vel_y * vel_z,
        vel_x * vel_z,
        (vel_y * vel_y - vel_z * vel_z) * vel_x,
        (vel_z * vel_z - vel_x * vel_x) * vel_y,
        (vel_x * vel_x - vel_y * vel_y) * vel_z,
    ]
    return np.stack(rows)


def relax_matrix():
    moments = moment_rows()
    scaled = moments.T / np.sum(moments * moments, axis=1)
    return (scaled @ (relax_rates[:, None] * moments)).astype(np.float32)


def column(values):
    return jnp.asarray(np.asarray(values, dtype=np.float32).reshape(-1, 1, 1, 1))


def plane_column(values):
    return jnp.asarray(np.asarray(values, dtype=np.float32).reshape(-1, 1, 1))


def expand(blocks):
    deep, tall, wide = blocks.shape
    big = jnp.broadcast_to(
        blocks[:, None, :, None, :, None], (deep, BLOCK, tall, BLOCK, wide, BLOCK)
    )
    return big.reshape(deep * BLOCK, tall * BLOCK, wide * BLOCK).astype(jnp.float32)


def collide(popul, solid):
    rho = jnp.sum(popul, axis=0)
    mom_x = jnp.sum(column(velocities[:, 0]) * popul, axis=0)
    mom_y = jnp.sum(column(velocities[:, 1]) * popul, axis=0)
    mom_z = jnp.sum(column(velocities[:, 2]) * popul, axis=0)
    inverse = 1.0 / rho
    vel_x = mom_x * inverse
    vel_y = mom_y * inverse
    vel_z = mom_z * inverse
    along = (
        column(velocities[:, 0]) * vel_x
        + column(velocities[:, 1]) * vel_y
        + column(velocities[:, 2]) * vel_z
    )
    speed_sq = vel_x * vel_x + vel_y * vel_y + vel_z * vel_z
    equil = (
        column(lattice_weights) * rho * (1.0 + 3.0 * along + 4.5 * along * along - 1.5 * speed_sq)
    )
    noneq = popul - equil
    relaxed = jnp.dot(
        jnp.asarray(relax_matrix()), noneq.reshape(19, -1), precision=lax.Precision.HIGHEST
    ).reshape(popul.shape)
    post = jnp.where(solid > 0, popul[opposite], popul - relaxed)
    fluid = 1.0 - solid
    stress = -(1.0 - 0.5 * visc_rate) * jnp.sum(
        column(velocities[:, 0] * velocities[:, 1]) * noneq, axis=0
    )
    return (post, jnp.stack([fluid * mom_x, fluid * stress]))


def assemble(shifted, le_top, le_bot):
    pieces = []
    for index in range(19):
        lift = velocities[index, 1]
        if lift == 0:
            pieces.append(shifted[index])
        elif lift > 0:
            pieces.append(
                jnp.concatenate([le_top[rising.index(index)][None], shifted[index, :-1]], axis=0)
            )
        else:
            pieces.append(
                jnp.concatenate([shifted[index, 1:], le_bot[falling.index(index)][None]], axis=0)
            )
    return jnp.stack(pieces)


def stream_across(post):
    depth_z = post.shape[2]
    width_x = post.shape[3]
    padded = extended(post, (("gx", 3), ("gz", 2)), 1)
    pieces = []
    for index in range(19):
        start_z = 1 - int(velocities[index, 2])
        start_x = 1 - int(velocities[index, 0])
        pieces.append(padded[index, :, start_z : start_z + depth_z, start_x : start_x + width_x])
    return jnp.stack(pieces)


def displaced_windows(planes, whole):
    width_x = planes.shape[3]
    count = lax.axis_size("gx")
    total = count * width_x
    offset_top = whole % total
    offset_bot = (total - whole - 1) % total
    full = lax.all_gather(planes, "gx", axis=3, tiled=True)
    doubled = jnp.concatenate([full, full[:, :, :, : width_x + 1]], axis=3)
    anchor = lax.axis_index("gx") * width_x
    start_top = (anchor + offset_top) % total
    start_bot = (anchor + offset_bot) % total
    win_top = lax.dynamic_slice_in_dim(doubled[0], start_top, width_x + 1, 2)
    win_bot = lax.dynamic_slice_in_dim(doubled[1], start_bot, width_x + 1, 2)
    return (win_top, win_bot)


def local(pop_ratio, solid_blocks, shift_whole, shift_frac):
    popul = pop_ratio * column(lattice_weights)
    solid = expand(solid_blocks)
    width_x = popul.shape[3]
    planes_y = popul.shape[1]
    accumulated = jnp.zeros((2,) + popul.shape[1:], jnp.float32)
    top_fix = plane_column(6.0 * lattice_weights[rising] * velocities[rising, 0] * wall_speed)
    bot_fix = plane_column(6.0 * lattice_weights[falling] * velocities[falling, 0] * wall_speed)
    for step in range(STEPS):
        post, fields = collide(popul, solid)
        accumulated = accumulated + fields
        shifted = stream_across(post)
        whole = shift_whole[step]
        weight = shift_frac[step].astype(jnp.float32) / fraction_unit
        planes = jnp.stack([shifted[np.array(rising), planes_y - 1], shifted[np.array(falling), 0]])
        win_top, win_bot = displaced_windows(planes, whole)
        le_top = (1.0 - weight) * win_top[:, :, :width_x] + weight * win_top[:, :, 1:] - top_fix
        le_bot = (1.0 - weight) * win_bot[:, :, 1:] + weight * win_bot[:, :, :width_x] + bot_fix
        popul = assemble(shifted, le_top, le_bot)
    profiles = lax.psum(jnp.sum(accumulated, axis=3), "gx")
    return (popul, accumulated, profiles)


def solution(mesh):
    return jax.shard_map(
        local,
        mesh=mesh,
        in_specs=(P(None, None, "gz", "gx"), P(None, "gz", "gx"), P(), P()),
        out_specs=(P(None, None, "gz", "gx"), P(None, None, "gz", "gx"), P(None, None, "gz")),
        check_vma=False,
    )
```

profile of v0, /device:TPU:0, one launch (start us, length us, event | category | flops | bytes accessed | tf_op | source)
XLA Modules:
  0.0 189.6 jit_solution(16554818729477392936)
XLA Ops:
  0.7 0.8 pad_clamp_fusion
  1.5 1.9 %multiply_reduce_fusion.6 = (f32[16,8,128]{2,1,0:T(8,128)S(1)}, f32[16,8,128]{2,1,0:T(8,128)S(1)}, f32[16,8,128]{2,1,0:T(8,128)S(1)}, f32[16,8,128]{2,1,0:T(8,128)S(1)}) fusion(f32[19]{0:T(128)} %constant.136, f32[19,16,8,128]{3,2,1,0:T(8,128)} %param.36, f32[19]{0:T(128)} %constant.134, f32[19]{0:T(128)} %constant.137, f32[19]{0:T(128)} %constant.138), kind=kLoop, calls=%fused_computation.42 | loop fusion | flops 2424832 | bytes 1507632 | tf_op jit(solution)/shard_map/reduce_sum | solution.py:131
  4.0 2.2 %fusion.17 = (f32[19,16,8,128]{3,2,1,0:T(8,128)S(1)}, f32[19,16,8,128]{3,2,1,0:T(8,128)}) fusion(f32[16,8,128]{2,1,0:T(8,128)S(1)} %get-tuple-element.47, f32[16,8,128]{2,1,0:T(8,128)S(1)} %get-tuple-element.50, f32[19]{0:T(128)S(1)} %copy-done.68, f32[16,8,128]{2,1,0:T(8,128)S(1)} %get-tuple-element.49, f32[19]{0:T(128)S(1)} %copy-done.65, ...), kind=kLoop, calls=%fused_computation.25 | loop fusion | flops 4669440 | bytes 4063536 | tf_op jit(solution)/shard_map/sub | solution.py:147
  6.4 0.9 copy-done.8
  7.3 0.9 copy.52
  8.2 1.4 fusion.92
  9.6 1.4 copy.53
  11.3 1.8 gt.9
  13.1 1.7 gather_fusion
  14.8 1.9 fusion.25
  16.6 1.5 fusion.85
  18.1 2.2 %copy.39 = f32[19,16,8,1]{0,2,3,1:T(8,128)S(1)} copy(f32[19,16,8,1]{3,2,1,0:T(8,128)} %get-tuple-element.90) | data formatting | bytes 19456 | tf_op jit(solution)/shard_map/slice | solution.py:70
  20.3 3.0 %collective-permute-start = (f32[19,16,8,1]{0,2,3,1:T(8,128)S(1)}, f32[19,16,8,1]{0,2,3,1:T(8,128)S(1)}, u32[]{:S(2)}, u32[]{:S(2)}) collective-permute-start(f32[19,16,8,1]{0,2,3,1:T(8,128)S(1)} %copy.39), channel_id=1, source_target_pairs={{0,8},{8,16},{16,24},{24,0},{1,9},{9,17},{17,25},{25,1},{2,10},{10... | collective-permute-start | bytes 29192 | tf_op jit(solution)/shard_map/ppermute | solution.py:72
  23.3 1.6 copy.41
  24.9 1.0 collective-permute-start.1
  33.8 2.3 %sub.117 = f32[1,16,8,128]{3,2,1,0:T(8,128)} reshape(f32[4,4,2,4,32,4]{5,4,3,2,1,0:T(8,128)S(1)} %broadcast_in_dim.49) | data formatting | bytes 131072 | tf_op jit(solution)/shard_map/sub | solution.py:152
  36.7 1.3 copy.40
  38.0 3.1 %copy.42 = f32[19,16,8,1]{3,2,1,0:T(8,128)} copy(f32[19,16,8,1]{0,2,3,1:T(8,128)} %collective-permute-done.1) | data formatting | bytes 19456 | tf_op jit(solution)/shard_map/ppermute | solution.py:73
  41.1 1.8 fusion.50
  42.8 2.0 %pad_maximum_fusion.3 = (f32[19,16,1,130]{3,2,1,0:T(1,128)S(1)}, f32[19,16,1,130]{3,2,1,0:T(1,128)S(1)}) fusion(f32[19,16,8,1]{3,2,1,0:T(8,128)S(1)} %copy-done.2, f32[19,16,8,128]{3,2,1,0:T(8,128)S(1)} %fusion.25, f32[19,16,8,1]{3,2,1,0:T(8,128)S(1)} %copy.40), kind=kLoop, calls=%fused_computation.59 | loop fusion | flops 158080 | bytes 1580800 | tf_op jit(solution)/shard_map/concatenate | solution.py:74
  44.8 0.7 constant_dynamic-update-slice_fusion.34
  45.6 0.8 constant_dynamic-update-slice_fusion.33
  46.3 2.5 %copy.71 = f32[19,16,8,128]{3,2,1,0:T(8,128)} copy(f32[19,16,8,128]{3,2,1,0:T(8,128)} %get-tuple-element.43) | data formatting | bytes 2490368
  48.8 3.5 %collective-permute-start.3 = (f32[19,16,1,130]{3,2,1,0:T(1,128)S(1)}, f32[19,16,1,130]{3,2,1,0:T(1,128)S(1)}, u32[]{:S(2)}, u32[]{:S(2)}) collective-permute-start(f32[19,16,1,130]{3,2,1,0:T(1,128)S(1)} %get-tuple-element.65), channel_id=1, source_target_pairs={{1,0},{2,1},{3,2},{4,3},{5,4},{6,5},{7,6},{0,7},{9,8},{10,9},{11,1... | collective-permute-start | bytes 474248 | tf_op jit(solution)/shard_map/ppermute | solution.py:73
  53.0 4.7 %collective-permute-done.2 = f32[19,16,1,130]{3,2,1,0:T(1,128)S(1)} collective-permute-done((f32[19,16,1,130]{3,2,1,0:T(1,128)S(1)}, f32[19,16,1,130]{3,2,1,0:T(1,128)S(1)}, u32[]{:S(2)}, u32[]{:S(2)}) %collective-permute-start.2) | collective-permute-done | bytes 158112 | tf_op jit(solution)/shard_map/ppermute | solution.py:72
  58.4 0.7 constant_dynamic-update-slice_fusion.11
  62.8 0.8 constant_dynamic-update-slice_fusion.5
  64.3 0.8 constant_dynamic-update-slice_fusion.3
  65.8 0.8 constant_dynamic-update-slice_fusion.1
  67.3 1.9 gather_fusion.2
  69.2 2.5 %gather_fusion.1 = f32[5,8,128]{2,1,0:T(8,128)} fusion(f32[19,16,8,128]{3,2,1,0:T(8,128)} %constant_dynamic-update-slice_fusion, s32[5]{0:T(128)S(1)} %copy-done.47), kind=kCustom, calls=%fused_computation.1 | custom fusion | bytes 41000 | tf_op jit(solution)/shard_map/gather | solution.py:218
  71.7 0.8 pad_maximum_fusion.48
  72.5 10.9 %all_gather.6 = f32[2,5,8,512]{3,2,1,0:T(8,128)S(1)} all-gather(f32[2,5,8,128]{3,2,1,0:T(8,128)S(1)} %pad_maximum_fusion.48), channel_id=1, replica_groups=mesh['gx'=4,'gz'=8] {'gx'}, dimensions={3}, use_global_device_ids=true | all-gather | bytes 204800 | tf_op jit(solution)/shard_map/all_gather | solution.py:194
  85.6 1.1 copy-done.4
  87.0 1.0 copy-done.5
  88.0 1.0 multiply_reduce_fusion.1
  89.1 2.2 %gather_fusion.3 = f32[19,16,8,128]{3,2,1,0:T(8,128)S(1)} fusion(f32[19,16,8,128]{3,2,1,0:T(8,128)} %copy-done.5, s32[1024]{0:T(1024)} %copy-done.71), kind=kCustom, calls=%fused_computation.3 | custom fusion | bytes 2490444 | tf_op jit(solution)/shard_map/gather | solution.py:151
  92.1 1.4 pad_maximum_fusion.23
  93.5 1.3 pad_maximum_fusion.25
  96.2 0.8 fusion.69
  97.7 6.3 %stack.178 = f32[19,16384]{1,0:T(8,128)} concatenate(f32[1,16384]{1,0:T(1,128)} %bitcast.276, f32[1,16384]{1,0:T(1,128)} %bitcast.272, f32[1,16384]{1,0:T(1,128)} %bitcast.273, f32[1,16384]{1,0:T(1,128)} %bitcast.277, f32[1,16384]{1,0:T(1,128)} %bitcast.279, f32[1,16384]{1,0:T(1,128)S(1)} %bitcast.264, f32[1,16384]{1,0:T(1,128)S(1)} %bitcast.265, f32[1,16384]{1,0:T(1,128)} %bitcast.278, ...), dimensions={0} | concatenate | bytes 2490368 | tf_op jit(solution)/shard_map/stack | solution.py:173
  104.1 3.5 %fusion.4 = f32[19,16384]{1,0:T(8,128)S(1)} fusion(f32[19,19]{1,0:T(8,128)S(1)} %copy-done.59, f32[19,16384]{1,0:T(8,128)} %stack.178, f32[16384]{0:T(1024)S(1)} %bitcast.274, f32[16384]{0:T(1024)S(1)} %get-tuple-element.93, f32[19]{0:T(128)S(1)} %copy-done.70, f32[16384]{0:T(1024)S(1)} %get-tuple-element.96, f32[19]{0:T(128)S(1)} %copy-done.67, ...), kind=kOutput, calls=%fused_computation.13 | convolution fusion | flops 75333632 | bytes 2819796 | tf_op jit(solution)/shard_map/dot_general | solution.py:148
  107.9 1.0 copy-done.6
  109.2 1.3 fusion.23
  110.5 1.5 fusion.83
  112.0 2.2 %copy.47 = f32[19,16,8,1]{0,2,3,1:T(8,128)S(1)} copy(f32[19,16,8,1]{3,2,1,0:T(8,128)} %get-tuple-element.82) | data formatting | bytes 19456 | tf_op jit(solution)/shard_map/slice | solution.py:71
  114.2 1.5 collective-permute-start.5
  115.7 1.0 copy.45
  117.9 16.0 %psum.7 = f32[2,16,8]{2,1,0:T(8,128)S(1)} all-reduce(f32[2,16,8]{2,1,0:T(8,128)S(1)} %get-tuple-element.15), channel_id=1, replica_groups=mesh['gx'=4,'gz'=8] {'gx'}, use_global_device_ids=true, to_apply=%region_10.11 | all-reduce | flops 256 | bytes 2048 | tf_op jit(solution)/shard_map/psum | solution.py:223
  134.6 1.3 copy.48
  135.9 2.2 %copy.46 = f32[19,16,8,1]{3,2,1,0:T(8,128)} copy(f32[19,16,8,1]{0,2,3,1:T(8,128)S(1)} %collective-permute-done.4) | data formatting | bytes 19456 | tf_op jit(solution)/shard_map/ppermute | solution.py:72
  138.1 1.6 pad_maximum_fusion.12
  139.7 0.8 fusion.46
  140.5 2.0 %pad_maximum_fusion = (f32[19,16,1,130]{3,2,1,0:T(1,128)S(1)}, f32[19,16,1,130]{3,2,1,0:T(1,128)S(1)}) fusion(f32[19,16,8,1]{3,2,1,0:T(8,128)S(1)} %copy.48, f32[19,16,8,128]{3,2,1,0:T(8,128)S(1)} %get-tuple-element.75, f32[19,16,8,1]{3,2,1,0:T(8,128)S(1)} %copy-done), kind=kLoop, calls=%fused_computation.56 | loop fusion | flops 158080 | bytes 1580800 | tf_op jit(solution)/shard_map/concatenate | solution.py:74
  143.8 2.4 %copy.103 = f32[19,16,8,128]{3,2,1,0:T(8,128)} copy(f32[19,16,8,128]{3,2,1,0:T(8,128)} %constant_dynamic-update-slice_fusion.69) | data formatting | bytes 2490368
  146.2 3.5 %collective-permute-start.7 = (f32[19,16,1,130]{3,2,1,0:T(1,128)S(1)}, f32[19,16,1,130]{3,2,1,0:T(1,128)S(1)}, u32[]{:S(2)}, u32[]{:S(2)}) collective-permute-start(f32[19,16,1,130]{3,2,1,0:T(1,128)S(1)} %get-tuple-element.61), channel_id=1, source_target_pairs={{1,0},{2,1},{3,2},{4,3},{5,4},{6,5},{7,6},{0,7},{9,8},{10,9},{11,1... | collective-permute-start | bytes 474248 | tf_op jit(solution)/shard_map/ppermute | solution.py:73
  150.4 5.4 %collective-permute-done.6 = f32[19,16,1,130]{3,2,1,0:T(1,128)S(1)} collective-permute-done((f32[19,16,1,130]{3,2,1,0:T(1,128)S(1)}, f32[19,16,1,130]{3,2,1,0:T(1,128)S(1)}, u32[]{:S(2)}, u32[]{:S(2)}) %collective-permute-start.6) | collective-permute-done | bytes 158112 | tf_op jit(solution)/shard_map/ppermute | solution.py:72
  160.8 0.7 constant_dynamic-update-slice_fusion.41
  162.3 0.8 constant_dynamic-update-slice_fusion.39
  163.7 0.8 constant_dynamic-update-slice_fusion.37
  165.3 1.9 gather_fusion.5
  167.1 2.5 %gather_fusion.4 = f32[5,8,128]{2,1,0:T(8,128)} fusion(f32[19,16,8,128]{3,2,1,0:T(8,128)} %constant_dynamic-update-slice_fusion.36, s32[5]{0:T(128)S(1)} %copy-done.47), kind=kCustom, calls=%fused_computation.4 | custom fusion | bytes 41000 | tf_op jit(solution)/shard_map/gather | solution.py:218
  169.6 0.8 pad_maximum_fusion.49
  170.4 8.3 %all_gather.7 = f32[2,5,8,512]{3,2,1,0:T(8,128)S(1)} all-gather(f32[2,5,8,128]{3,2,1,0:T(8,128)S(1)} %pad_maximum_fusion.49), channel_id=1, replica_groups=mesh['gx'=4,'gz'=8] {'gx'}, dimensions={3}, use_global_device_ids=true | all-gather | bytes 204800 | tf_op jit(solution)/shard_map/all_gather | solution.py:194
  (253 shorter events, 37.7 us)
Async XLA Ops:
  0.6 3.4 %copy-start.60 = (f32[19]{0:T(128)S(1)}, f32[19]{0:T(128)}, u32[]{:S(2)}) copy-start(f32[19]{0:T(128)} %constant.136) | copy-start | bytes 232
  0.6 3.4 %copy-start.63 = (f32[19]{0:T(128)S(1)}, f32[19]{0:T(128)}, u32[]{:S(2)}) copy-start(f32[19]{0:T(128)} %constant.134) | copy-start | bytes 232
  0.7 3.4 %copy-start.65 = (f32[19]{0:T(128)S(1)}, f32[19]{0:T(128)}, u32[]{:S(2)}) copy-start(f32[19]{0:T(128)} %constant.137) | copy-start | bytes 232
  0.7 3.4 %copy-start.68 = (f32[19]{0:T(128)S(1)}, f32[19]{0:T(128)}, u32[]{:S(2)}) copy-start(f32[19]{0:T(128)} %constant.138) | copy-start | bytes 232
  0.7 3.3 %copy-start.7 = (f32[19,16,8,128]{3,2,1,0:T(8,128)S(1)}, f32[19,16,8,128]{3,2,1,0:T(8,128)}, u32[]{:S(2)}) copy-start(f32[19,16,8,128]{3,2,1,0:T(8,128)} %param.36) | copy-start | bytes 3735556
  1.5 11.6 %copy-start.71 = (s32[1024]{0:T(1024)}, s32[1024]{0:T(1024)S(1)}, u32[]{:S(2)}) copy-start(s32[1024]{0:T(1024)S(1)} %pad_clamp_fusion) | copy-start | bytes 12292
  9.6 3.5 %copy-start.10 = (f32[19,16,8,128]{3,2,1,0:T(8,128)S(1)}, f32[19,16,8,128]{3,2,1,0:T(8,128)}, u32[]{:S(2)}) copy-start(f32[19,16,8,128]{3,2,1,0:T(8,128)} %get-tuple-element.74) | copy-start | bytes 3735556
  18.1 8.4 %copy-start.75 = (s32[2]{0:T(128)S(1)}, s32[2]{0:T(128)}, u32[]{:S(2)}) copy-start(s32[2]{0:T(128)} %param.38) | copy-start | bytes 28
  18.1 9.0 %copy-start.76 = (s32[2]{0:T(128)S(1)}, s32[2]{0:T(128)}, u32[]{:S(2)}) copy-start(s32[2]{0:T(128)} %param.39) | copy-start | bytes 28
  20.3 16.4 %collective-permute-start = (f32[19,16,8,1]{0,2,3,1:T(8,128)S(1)}, f32[19,16,8,1]{0,2,3,1:T(8,128)S(1)}, u32[]{:S(2)}, u32[]{:S(2)}) collective-permute-start(f32[19,16,8,1]{0,2,3,1:T(8,128)S(1)} %copy.39), channel_id=1, source_target_pairs={{0,8},{8,16},{16,24},{24,0},{1,9},{9,17},{17,25},{25,1},{2,10},{10... | collective-permute-start | bytes 29192 | tf_op jit(solution)/shard_map/ppermute | solution.py:72
  24.9 13.1 %collective-permute-start.1 = (f32[19,16,8,1]{0,2,3,1:T(8,128)}, f32[19,16,8,1]{0,2,3,1:T(8,128)}, u32[]{:S(2)}, u32[]{:S(2)}) collective-permute-start(f32[19,16,8,1]{0,2,3,1:T(8,128)} %copy.41), channel_id=1, source_target_pairs={{8,0},{16,8},{24,16},{0,24},{9,1},{17,9},{25,17},{1,25},{10,2},{18... | collective-permute-start | bytes 29192 | tf_op jit(solution)/shard_map/ppermute | solution.py:73
  41.1 1.8 copy-start.2
  48.8 8.9 %collective-permute-start.2 = (f32[19,16,1,130]{3,2,1,0:T(1,128)S(1)}, f32[19,16,1,130]{3,2,1,0:T(1,128)S(1)}, u32[]{:S(2)}, u32[]{:S(2)}) collective-permute-start(f32[19,16,1,130]{3,2,1,0:T(1,128)S(1)} %get-tuple-element.66), channel_id=1, source_target_pairs={{0,1},{1,2},{2,3},{3,4},{4,5},{5,6},{6,7},{7,0},{8,9},{9,10},{10,1... | collective-permute-start | bytes 474248 | tf_op jit(solution)/shard_map/ppermute | solution.py:72
  48.8 9.6 %collective-permute-start.3 = (f32[19,16,1,130]{3,2,1,0:T(1,128)S(1)}, f32[19,16,1,130]{3,2,1,0:T(1,128)S(1)}, u32[]{:S(2)}, u32[]{:S(2)}) collective-permute-start(f32[19,16,1,130]{3,2,1,0:T(1,128)S(1)} %get-tuple-element.65), channel_id=1, source_target_pairs={{1,0},{2,1},{3,2},{4,3},{5,4},{6,5},{7,6},{0,7},{9,8},{10,9},{11,1... | collective-permute-start | bytes 474248 | tf_op jit(solution)/shard_map/ppermute | solution.py:73
  66.6 2.6 %copy-start.47 = (s32[5]{0:T(128)S(1)}, s32[5]{0:T(128)}, u32[]{:S(2)}) copy-start(s32[5]{0:T(128)} %constant.208) | copy-start | bytes 64
  67.3 17.1 %copy-start.72 = (f32[5]{0:T(128)S(1)}, f32[5]{0:T(128)}, u32[]{:S(2)}) copy-start(f32[5]{0:T(128)} %constant.144) | copy-start | bytes 64
  71.7 12.9 %copy-start.17 = (f32[15,8,128]{2,1,0:T(8,128)S(1)}, f32[15,8,128]{2,1,0:T(8,128)}, u32[]{:S(2)}) copy-start(f32[15,8,128]{2,1,0:T(8,128)} %get-tuple-element.88) | copy-start | bytes 184324
  71.7 13.5 %copy-start.3 = (f32[19,16,8,1]{3,2,1,0:T(8,128)S(1)}, f32[19,16,8,1]{3,2,1,0:T(8,128)}, u32[]{:S(2)}) copy-start(f32[19,16,8,1]{3,2,1,0:T(8,128)} %copy.42) | copy-start | bytes 29188
  84.6 2.2 %copy-start.53 = (f32[1,8,128]{2,1,0:T(8,128)}, f32[1,8,128]{2,1,0:T(8,128)S(1)}, u32[]{:S(2)}) copy-start(f32[1,8,128]{2,1,0:T(8,128)S(1)} %get-tuple-element.114) | copy-start | bytes 12292
  84.6 2.2 %copy-start.51 = (f32[1,8,128]{2,1,0:T(8,128)}, f32[1,8,128]{2,1,0:T(8,128)S(1)}, u32[]{:S(2)}) copy-start(f32[1,8,128]{2,1,0:T(8,128)S(1)} %get-tuple-element.113) | copy-start | bytes 12292
  84.6 2.3 %copy-start.49 = (f32[1,8,128]{2,1,0:T(8,128)}, f32[1,8,128]{2,1,0:T(8,128)S(1)}, u32[]{:S(2)}) copy-start(f32[1,8,128]{2,1,0:T(8,128)S(1)} %get-tuple-element.112) | copy-start | bytes 12292
  85.5 2.5 %copy-start.61 = (f32[19]{0:T(128)S(1)}, f32[19]{0:T(128)}, u32[]{:S(2)}) copy-start(f32[19]{0:T(128)} %constant.136) | copy-start | bytes 232
  85.5 2.5 %copy-start.66 = (f32[19]{0:T(128)S(1)}, f32[19]{0:T(128)}, u32[]{:S(2)}) copy-start(f32[19]{0:T(128)} %constant.137) | copy-start | bytes 232
  85.5 2.5 %copy-start.69 = (f32[19]{0:T(128)S(1)}, f32[19]{0:T(128)}, u32[]{:S(2)}) copy-start(f32[19]{0:T(128)} %constant.138) | copy-start | bytes 232
  89.0 2.3 %copy-start.16 = (f32[15,8,128]{2,1,0:T(8,128)S(1)}, f32[15,8,128]{2,1,0:T(8,128)}, u32[]{:S(2)}) copy-start(f32[15,8,128]{2,1,0:T(8,128)} %get-tuple-element.87) | copy-start | bytes 184324
  89.0 2.3 %copy-start.18 = (f32[15,8,128]{2,1,0:T(8,128)S(1)}, f32[15,8,128]{2,1,0:T(8,128)}, u32[]{:S(2)}) copy-start(f32[15,8,128]{2,1,0:T(8,128)} %get-tuple-element.88) | copy-start | bytes 184324
  89.0 3.0 %copy-start.28 = (f32[15,8,128]{2,1,0:T(8,128)S(1)}, f32[15,8,128]{2,1,0:T(8,128)}, u32[]{:S(2)}) copy-start(f32[15,8,128]{2,1,0:T(8,128)} %copy-done.27) | copy-start | bytes 184324
  89.1 3.0 %copy-start.30 = (f32[15,8,128]{2,1,0:T(8,128)S(1)}, f32[15,8,128]{2,1,0:T(8,128)}, u32[]{:S(2)}) copy-start(f32[15,8,128]{2,1,0:T(8,128)} %copy-done.29) | copy-start | bytes 184324
  89.1 3.0 %copy-start.52 = (f32[1,8,128]{2,1,0:T(8,128)S(1)}, f32[1,8,128]{2,1,0:T(8,128)}, u32[]{:S(2)}) copy-start(f32[1,8,128]{2,1,0:T(8,128)} %copy-done.51) | copy-start | bytes 12292
  89.1 4.4 %copy-start.12 = (f32[15,8,128]{2,1,0:T(8,128)S(1)}, f32[15,8,128]{2,1,0:T(8,128)}, u32[]{:S(2)}) copy-start(f32[15,8,128]{2,1,0:T(8,128)} %get-tuple-element.71) | copy-start | bytes 184324
  89.1 4.4 %copy-start.14 = (f32[15,8,128]{2,1,0:T(8,128)S(1)}, f32[15,8,128]{2,1,0:T(8,128)}, u32[]{:S(2)}) copy-start(f32[15,8,128]{2,1,0:T(8,128)} %get-tuple-element.72) | copy-start | bytes 184324
  89.1 5.7 %copy-start.22 = (f32[15,8,128]{2,1,0:T(8,128)S(1)}, f32[15,8,128]{2,1,0:T(8,128)}, u32[]{:S(2)}) copy-start(f32[15,8,128]{2,1,0:T(8,128)} %copy-done.21) | copy-start | bytes 184324
  89.1 5.7 %copy-start.26 = (f32[15,8,128]{2,1,0:T(8,128)S(1)}, f32[15,8,128]{2,1,0:T(8,128)}, u32[]{:S(2)}) copy-start(f32[15,8,128]{2,1,0:T(8,128)} %copy-done.25) | copy-start | bytes 184324
  89.1 6.4 %copy-start.20 = (f32[15,8,128]{2,1,0:T(8,128)S(1)}, f32[15,8,128]{2,1,0:T(8,128)}, u32[]{:S(2)}) copy-start(f32[15,8,128]{2,1,0:T(8,128)} %copy-done.19) | copy-start | bytes 184324
  89.1 6.4 %copy-start.24 = (f32[15,8,128]{2,1,0:T(8,128)S(1)}, f32[15,8,128]{2,1,0:T(8,128)}, u32[]{:S(2)}) copy-start(f32[15,8,128]{2,1,0:T(8,128)} %copy-done.23) | copy-start | bytes 184324
  89.1 6.4 %copy-start.50 = (f32[1,8,128]{2,1,0:T(8,128)S(1)}, f32[1,8,128]{2,1,0:T(8,128)}, u32[]{:S(2)}) copy-start(f32[1,8,128]{2,1,0:T(8,128)} %copy-done.49) | copy-start | bytes 12292
  91.3 4.8 %copy-start.35 = (f32[16,8,128]{2,1,0:T(8,128)S(1)}, f32[16,8,128]{2,1,0:T(8,128)}, u32[]{:S(2)}) copy-start(f32[16,8,128]{2,1,0:T(8,128)} %get-tuple-element.12) | copy-start | bytes 196612
  91.3 4.8 %copy-start.38 = (f32[1,16,8,128]{3,2,1,0:T(8,128)S(1)}, f32[1,16,8,128]{3,2,1,0:T(8,128)}, u32[]{:S(2)}) copy-start(f32[1,16,8,128]{3,2,1,0:T(8,128)} %get-tuple-element.46) | copy-start | bytes 196612
  91.3 4.8 %copy-start.39 = (f32[1,16,8,128]{3,2,1,0:T(8,128)S(1)}, f32[1,16,8,128]{3,2,1,0:T(8,128)}, u32[]{:S(2)}) copy-start(f32[1,16,8,128]{3,2,1,0:T(8,128)} %get-tuple-element.44) | copy-start | bytes 196612
  91.4 4.8 %copy-start.54 = (f32[1,8,128]{2,1,0:T(8,128)S(1)}, f32[1,8,128]{2,1,0:T(8,128)}, u32[]{:S(2)}) copy-start(f32[1,8,128]{2,1,0:T(8,128)} %copy-done.53) | copy-start | bytes 12292
  91.4 4.8 %copy-start.56 = (f32[1,8,128]{2,1,0:T(8,128)S(1)}, f32[1,8,128]{2,1,0:T(8,128)}, u32[]{:S(2)}) copy-start(f32[1,8,128]{2,1,0:T(8,128)} %copy-done.55) | copy-start | bytes 12292
  92.0 5.5 %copy-start.33 = (f32[1,16,8,128]{3,2,1,0:T(8,128)S(1)}, f32[1,16,8,128]{3,2,1,0:T(8,128)}, u32[]{:S(2)}) copy-start(f32[1,16,8,128]{3,2,1,0:T(8,128)} %sub.117) | copy-start | bytes 196612
  92.1 5.5 %copy-start.37 = (f32[16,8,128]{2,1,0:T(8,128)S(1)}, f32[16,8,128]{2,1,0:T(8,128)}, u32[]{:S(2)}) copy-start(f32[16,8,128]{2,1,0:T(8,128)} %copy-done.36) | copy-start | bytes 196612
  92.1 5.5 %copy-start.41 = (f32[16,8,128]{2,1,0:T(8,128)S(1)}, f32[16,8,128]{2,1,0:T(8,128)}, u32[]{:S(2)}) copy-start(f32[16,8,128]{2,1,0:T(8,128)} %get-tuple-element.10) | copy-start | bytes 196612
  92.1 5.5 %copy-start.42 = (f32[16,8,128]{2,1,0:T(8,128)S(1)}, f32[16,8,128]{2,1,0:T(8,128)}, u32[]{:S(2)}) copy-start(f32[16,8,128]{2,1,0:T(8,128)} %get-tuple-element.11) | copy-start | bytes 196612
  97.6 6.4 %copy-start.32 = (f32[1,16,8,128]{3,2,1,0:T(8,128)S(1)}, f32[1,16,8,128]{3,2,1,0:T(8,128)}, u32[]{:S(2)}) copy-start(f32[1,16,8,128]{3,2,1,0:T(8,128)} %copy-done.31) | copy-start | bytes 196612
  97.6 6.4 %copy-start.59 = (f32[19,19]{1,0:T(8,128)S(1)}, f32[19,19]{1,0:T(8,128)}, u32[]{:S(2)}) copy-start(f32[19,19]{1,0:T(8,128)} %constant.119.clone) | copy-start | bytes 4336
  97.6 6.4 %copy-start.62 = (f32[19]{0:T(128)S(1)}, f32[19]{0:T(128)}, u32[]{:S(2)}) copy-start(f32[19]{0:T(128)} %constant.136) | copy-start | bytes 232
  97.6 6.4 %copy-start.64 = (f32[19]{0:T(128)S(1)}, f32[19]{0:T(128)}, u32[]{:S(2)}) copy-start(f32[19]{0:T(128)} %constant.134) | copy-start | bytes 232
  97.7 6.4 %copy-start.67 = (f32[19]{0:T(128)S(1)}, f32[19]{0:T(128)}, u32[]{:S(2)}) copy-start(f32[19]{0:T(128)} %constant.137) | copy-start | bytes 232
  97.7 6.4 %copy-start.70 = (f32[19]{0:T(128)S(1)}, f32[19]{0:T(128)}, u32[]{:S(2)}) copy-start(f32[19]{0:T(128)} %constant.138) | copy-start | bytes 232
  107.6 1.7 copy-start.9
  112.0 5.2 %copy-start.34 = (f32[1,16,8,128]{3,2,1,0:T(8,128)S(1)}, f32[1,16,8,128]{3,2,1,0:T(8,128)}, u32[]{:S(2)}) copy-start(f32[1,16,8,128]{3,2,1,0:T(8,128)} %sub.117) | copy-start | bytes 196612
  114.2 20.4 %collective-permute-start.5 = (f32[19,16,8,1]{0,2,3,1:T(8,128)S(1)}, f32[19,16,8,1]{0,2,3,1:T(8,128)S(1)}, u32[]{:S(2)}, u32[]{:S(2)}) collective-permute-start(f32[19,16,8,1]{0,2,3,1:T(8,128)S(1)} %copy.47), channel_id=1, source_target_pairs={{8,0},{16,8},{24,16},{0,24},{9,1},{17,9},{25,17},{1,25},{10,2},{18... | collective-permute-start | bytes 29192 | tf_op jit(solution)/shard_map/ppermute | solution.py:73
  116.7 19.2 %collective-permute-start.4 = (f32[19,16,8,1]{0,2,3,1:T(8,128)S(1)}, f32[19,16,8,1]{0,2,3,1:T(8,128)S(1)}, u32[]{:S(2)}, u32[]{:S(2)}) collective-permute-start(f32[19,16,8,1]{0,2,3,1:T(8,128)S(1)} %copy.45), channel_id=1, source_target_pairs={{0,8},{8,16},{16,24},{24,0},{1,9},{9,17},{17,25},{25,1},{2,10},{10... | collective-permute-start | bytes 29192 | tf_op jit(solution)/shard_map/ppermute | solution.py:72
  146.2 9.6 %collective-permute-start.6 = (f32[19,16,1,130]{3,2,1,0:T(1,128)S(1)}, f32[19,16,1,130]{3,2,1,0:T(1,128)S(1)}, u32[]{:S(2)}, u32[]{:S(2)}) collective-permute-start(f32[19,16,1,130]{3,2,1,0:T(1,128)S(1)} %get-tuple-element.62), channel_id=1, source_target_pairs={{0,1},{1,2},{2,3},{3,4},{4,5},{5,6},{6,7},{7,0},{8,9},{9,10},{10,1... | collective-permute-start | bytes 474248 | tf_op jit(solution)/shard_map/ppermute | solution.py:72
  146.2 10.3 %collective-permute-start.7 = (f32[19,16,1,130]{3,2,1,0:T(1,128)S(1)}, f32[19,16,1,130]{3,2,1,0:T(1,128)S(1)}, u32[]{:S(2)}, u32[]{:S(2)}) collective-permute-start(f32[19,16,1,130]{3,2,1,0:T(1,128)S(1)} %get-tuple-element.61), channel_id=1, source_target_pairs={{1,0},{2,1},{3,2},{4,3},{5,4},{6,5},{7,6},{0,7},{9,8},{10,9},{11,1... | collective-permute-start | bytes 474248 | tf_op jit(solution)/shard_map/ppermute | solution.py:73
  164.5 14.3 %copy-start.74 = (f32[5]{0:T(128)S(1)}, f32[5]{0:T(128)}, u32[]{:S(2)}) copy-start(f32[5]{0:T(128)} %constant.146) | copy-start | bytes 64
  165.3 13.8 %copy-start.73 = (f32[5]{0:T(128)S(1)}, f32[5]{0:T(128)}, u32[]{:S(2)}) copy-start(f32[5]{0:T(128)} %constant.144) | copy-start | bytes 64
  169.6 9.6 %copy-start.46 = (f32[15,8,128]{2,1,0:T(8,128)S(1)}, f32[15,8,128]{2,1,0:T(8,128)}, u32[]{:S(2)}) copy-start(f32[15,8,128]{2,1,0:T(8,128)} %get-tuple-element.78) | copy-start | bytes 184324
  169.6 10.2 %copy-start.1 = (f32[19,16,8,1]{3,2,1,0:T(8,128)S(1)}, f32[19,16,8,1]{3,2,1,0:T(8,128)}, u32[]{:S(2)}) copy-start(f32[19,16,8,1]{3,2,1,0:T(8,128)} %copy.46) | copy-start | bytes 29188
  179.8 2.1 %copy-start.45 = (f32[15,8,128]{2,1,0:T(8,128)S(1)}, f32[15,8,128]{2,1,0:T(8,128)}, u32[]{:S(2)}) copy-start(f32[15,8,128]{2,1,0:T(8,128)} %get-tuple-element.77) | copy-start | bytes 184324
  179.8 2.8 %copy-start.44 = (f32[15,8,128]{2,1,0:T(8,128)S(1)}, f32[15,8,128]{2,1,0:T(8,128)}, u32[]{:S(2)}) copy-start(f32[15,8,128]{2,1,0:T(8,128)} %get-tuple-element.69) | copy-start | bytes 184324
  179.8 4.0 %copy-start.43 = (f32[15,8,128]{2,1,0:T(8,128)S(1)}, f32[15,8,128]{2,1,0:T(8,128)}, u32[]{:S(2)}) copy-start(f32[15,8,128]{2,1,0:T(8,128)} %get-tuple-element.68) | copy-start | bytes 184324
  (22 other events, 28.3 us)
where the time goes:
time: 191 us; the launch traced here: 190 us
  local copies, waits for them, and re-layouts  63.7 us (33%)
  other arithmetic  54.5 us (29%)
  blocking collectives  35.1 us (18%)
  starting transfers between devices  13.1 us (7%)
  waiting for transfers between devices  10.1 us (5%)
  between operations  8.13 us (4%)
  matrix products  4.87 us (3%)
    unnamed x44, other arithmetic  25.5 us
    unnamed x179, local copies, waits for them, and re-layouts  20.6 us
    all_gather x2, blocking collectives, displaced_windows(): full = lax.all_gather(planes, 'gx', axis=3, tiled=True)  19.2 us
    psum x1, blocking collectives, local(): profiles = lax.psum(jnp.sum(accumulated, axis=3), 'gx')  16 us
    ppermute x4, waiting for transfers between devices, extended(): before = lax.ppermute(last, axis, up)  10.1 us
    ppermute x4, starting transfers between devices, extended(): after = lax.ppermute(initial, axis, down)  9.53 us
    slice x4, local copies, waits for them, and re-layouts, extended(): initial = lax.slice_in_dim(value, 0, width, axis=dim)  6.71 us
    another operation x1, local copies, waits for them, and re-layouts, assemble(): return jnp.stack(pieces)  6.33 us
  transfers between devices with their start and end apart: 8, of which 2 were waited for; matrix products, arithmetic and copies ran while one was open for 7% of the time, Pallas kernels for 0%

commit v1 on v0

--- a/solution.py
+++ b/solution.py
@@ -220,7 +220,7 @@
         le_top = (1.0 - weight) * win_top[:, :, :width_x] + weight * win_top[:, :, 1:] - top_fix
         le_bot = (1.0 - weight) * win_bot[:, :, 1:] + weight * win_bot[:, :, :width_x] + bot_fix
         popul = assemble(shifted, le_top, le_bot)
-    profiles = lax.psum(jnp.sum(accumulated, axis=3), "gx")
+    profiles = jnp.sum(lax.all_gather(jnp.sum(accumulated, axis=3), "gx"), axis=0)
     return (popul, accumulated, profiles)
 
 

time: 191 us -> 184 us (0.963)
  blocking collectives: 35.1 us -> 28.5 us
    psum x1 -> x0, blocking collectives: 16 us -> none  [local(): profiles = lax.psum(jnp.sum(accumulated, axis=3), 'gx')]
    all_gather x0 -> x1, blocking collectives: none -> 8.42 us  [local(): lax.all_gather(jnp.sum(accumulated, axis=3), 'gx')]
    unnamed x179 -> x178, local copies, waits for them, and re-layouts: 20.6 us -> 20 us
where the time goes in v1:
time: 184 us; the launch traced here: 183 us
  local copies, waits for them, and re-layouts  63.1 us (34%)
  other arithmetic  55.1 us (30%)
  blocking collectives  28.5 us (15%)
  starting transfers between devices  13.1 us (7%)
  waiting for transfers between devices  10.1 us (5%)
  between operations  8.13 us (4%)
  matrix products  4.87 us (3%)
    unnamed x44, other arithmetic  25.5 us
    all_gather x2, blocking collectives, displaced_windows(): full = lax.all_gather(planes, 'gx', axis=3, tiled=True)  20.1 us
    unnamed x178, local copies, waits for them, and re-layouts  20 us
    ppermute x4, waiting for transfers between devices, extended(): before = lax.ppermute(last, axis, up)  10.1 us
    ppermute x4, starting transfers between devices, extended(): after = lax.ppermute(initial, axis, down)  9.53 us
    all_gather x1, blocking collectives, local(): lax.all_gather(jnp.sum(accumulated, axis=3), 'gx')  8.42 us
    slice x4, local copies, waits for them, and re-layouts, extended(): initial = lax.slice_in_dim(value, 0, width, axis=dim)  6.71 us
    another operation x1, local copies, waits for them, and re-layouts, assemble(): return jnp.stack(pieces)  6.33 us
  transfers between devices with their start and end apart: 8, of which 2 were waited for; matrix products, arithmetic and copies ran while one was open for 7% of the time, Pallas kernels for 0%

profile of v1, /device:TPU:0, one launch (start us, length us, event | category | flops | bytes accessed | tf_op | source)
XLA Modules:
  0.0 182.9 jit_solution(4255828108452994812)
XLA Ops:
  0.7 0.8 pad_clamp_fusion
  1.5 1.9 %multiply_reduce_fusion.6 = (f32[16,8,128]{2,1,0:T(8,128)S(1)}, f32[16,8,128]{2,1,0:T(8,128)S(1)}, f32[16,8,128]{2,1,0:T(8,128)S(1)}, f32[16,8,128]{2,1,0:T(8,128)S(1)}) fusion(f32[19]{0:T(128)} %constant.136, f32[19,16,8,128]{3,2,1,0:T(8,128)} %param.36, f32[19]{0:T(128)} %constant.134, f32[19]{0:T(128)} %constant.137, f32[19]{0:T(128)} %constant.138), kind=kLoop, calls=%fused_computation.42 | loop fusion | flops 2424832 | bytes 1507632 | tf_op jit(solution)/shard_map/reduce_sum | solution.py:131
  4.0 2.2 %fusion.17 = (f32[19,16,8,128]{3,2,1,0:T(8,128)S(1)}, f32[19,16,8,128]{3,2,1,0:T(8,128)}) fusion(f32[16,8,128]{2,1,0:T(8,128)S(1)} %get-tuple-element.44, f32[16,8,128]{2,1,0:T(8,128)S(1)} %get-tuple-element.47, f32[19]{0:T(128)S(1)} %copy-done.68, f32[16,8,128]{2,1,0:T(8,128)S(1)} %get-tuple-element.46, f32[19]{0:T(128)S(1)} %copy-done.65, ...), kind=kLoop, calls=%fused_computation.25 | loop fusion | flops 4669440 | bytes 4063536 | tf_op jit(solution)/shard_map/sub | solution.py:147
  6.4 0.9 copy-done.8
  7.3 0.9 copy.64
  8.2 1.4 fusion.92
  9.6 1.4 copy.65
  11.3 1.8 gt.9
  13.1 1.7 gather_fusion
  14.8 1.9 %fusion.25 = f32[19,16,8,128]{3,2,1,0:T(8,128)S(1)} fusion(f32[19,16,8,128]{3,2,1,0:T(8,128)} %gather_fusion, f32[24,128,128]{2,1,0:T(8,128)} %bitcast.263, pred[16,8,128]{2,1,0:T(8,128)(4,1)S(1)} %gt.9, f32[19,16,8,128]{3,2,1,0:T(8,128)S(1)} %copy-done.7, f32[19]{0:T(128)S(1)} %copy-done.63), kind=kLoop, calls=%fused_computation.35 | loop fusion | flops 933888 | bytes 4997196 | tf_op jit(solution)/shard_map/jit(_where)/select_n | solution.py:151
  16.6 1.5 fusion.85
  18.1 2.2 %copy.51 = f32[19,16,8,1]{0,2,3,1:T(8,128)S(1)} copy(f32[19,16,8,1]{3,2,1,0:T(8,128)} %get-tuple-element.87) | data formatting | bytes 19456 | tf_op jit(solution)/shard_map/slice | solution.py:70
  20.3 3.0 %collective-permute-start = (f32[19,16,8,1]{0,2,3,1:T(8,128)S(1)}, f32[19,16,8,1]{0,2,3,1:T(8,128)S(1)}, u32[]{:S(2)}, u32[]{:S(2)}) collective-permute-start(f32[19,16,8,1]{0,2,3,1:T(8,128)S(1)} %copy.51), channel_id=1, source_target_pairs={{0,8},{8,16},{16,24},{24,0},{1,9},{9,17},{17,25},{25,1},{2,10},{10... | collective-permute-start | bytes 29192 | tf_op jit(solution)/shard_map/ppermute | solution.py:72
  23.3 1.6 copy.53
  24.9 1.0 collective-permute-start.1
  33.8 2.3 %sub.117 = f32[1,16,8,128]{3,2,1,0:T(8,128)} reshape(f32[4,4,2,4,32,4]{5,4,3,2,1,0:T(8,128)S(1)} %broadcast_in_dim.49) | data formatting | bytes 131072 | tf_op jit(solution)/shard_map/sub | solution.py:152
  36.7 1.3 copy.52
  38.0 3.1 %copy.54 = f32[19,16,8,1]{3,2,1,0:T(8,128)} copy(f32[19,16,8,1]{0,2,3,1:T(8,128)} %collective-permute-done.1) | data formatting | bytes 19456 | tf_op jit(solution)/shard_map/ppermute | solution.py:73
  41.1 1.8 fusion.50
  42.8 2.0 %pad_maximum_fusion.3 = (f32[19,16,1,130]{3,2,1,0:T(1,128)S(1)}, f32[19,16,1,130]{3,2,1,0:T(1,128)S(1)}) fusion(f32[19,16,8,1]{3,2,1,0:T(8,128)S(1)} %copy-done.2, f32[19,16,8,128]{3,2,1,0:T(8,128)S(1)} %fusion.25, f32[19,16,8,1]{3,2,1,0:T(8,128)S(1)} %copy.52), kind=kLoop, calls=%fused_computation.59 | loop fusion | flops 158080 | bytes 1580800 | tf_op jit(solution)/shard_map/concatenate | solution.py:74
  44.8 0.7 constant_dynamic-update-slice_fusion.34
  45.6 0.8 constant_dynamic-update-slice_fusion.33
  46.3 2.5 %copy.83 = f32[19,16,8,128]{3,2,1,0:T(8,128)} copy(f32[19,16,8,128]{3,2,1,0:T(8,128)} %get-tuple-element.40) | data formatting | bytes 2490368
  48.8 3.5 %collective-permute-start.3 = (f32[19,16,1,130]{3,2,1,0:T(1,128)S(1)}, f32[19,16,1,130]{3,2,1,0:T(1,128)S(1)}, u32[]{:S(2)}, u32[]{:S(2)}) collective-permute-start(f32[19,16,1,130]{3,2,1,0:T(1,128)S(1)} %get-tuple-element.62), channel_id=1, source_target_pairs={{1,0},{2,1},{3,2},{4,3},{5,4},{6,5},{7,6},{0,7},{9,8},{10,9},{11,1... | collective-permute-start | bytes 474248 | tf_op jit(solution)/shard_map/ppermute | solution.py:73
  53.0 4.7 %collective-permute-done.2 = f32[19,16,1,130]{3,2,1,0:T(1,128)S(1)} collective-permute-done((f32[19,16,1,130]{3,2,1,0:T(1,128)S(1)}, f32[19,16,1,130]{3,2,1,0:T(1,128)S(1)}, u32[]{:S(2)}, u32[]{:S(2)}) %collective-permute-start.2) | collective-permute-done | bytes 158112 | tf_op jit(solution)/shard_map/ppermute | solution.py:72
  58.4 0.7 constant_dynamic-update-slice_fusion.11
  62.8 0.8 constant_dynamic-update-slice_fusion.5
  64.3 0.8 constant_dynamic-update-slice_fusion.3
  65.8 0.8 constant_dynamic-update-slice_fusion.1
  67.3 1.9 %gather_fusion.2 = f32[5,8,128]{2,1,0:T(8,128)S(1)} fusion(f32[19,16,8,128]{3,2,1,0:T(8,128)} %constant_dynamic-update-slice_fusion, s32[5]{0:T(128)S(1)} %copy-done.48), kind=kCustom, calls=%fused_computation.2 | custom fusion | bytes 41000 | tf_op jit(solution)/shard_map/gather | solution.py:218
  69.2 2.5 %gather_fusion.1 = f32[5,8,128]{2,1,0:T(8,128)} fusion(f32[19,16,8,128]{3,2,1,0:T(8,128)} %constant_dynamic-update-slice_fusion, s32[5]{0:T(128)S(1)} %copy-done.47), kind=kCustom, calls=%fused_computation.1 | custom fusion | bytes 41000 | tf_op jit(solution)/shard_map/gather | solution.py:218
  71.7 0.8 pad_maximum_fusion.48
  72.5 10.9 %all_gather.12 = f32[2,5,8,512]{3,2,1,0:T(8,128)S(1)} all-gather(f32[2,5,8,128]{3,2,1,0:T(8,128)S(1)} %pad_maximum_fusion.48), channel_id=1, replica_groups=mesh['gx'=4,'gz'=8] {'gx'}, dimensions={3}, use_global_device_ids=true | all-gather | bytes 204800 | tf_op jit(solution)/shard_map/all_gather | solution.py:194
  85.6 1.1 copy-done.4
  87.0 1.0 copy-done.5
  88.0 1.0 multiply_reduce_fusion.1
  89.1 2.2 %gather_fusion.3 = f32[19,16,8,128]{3,2,1,0:T(8,128)S(1)} fusion(f32[19,16,8,128]{3,2,1,0:T(8,128)} %copy-done.5, s32[1024]{0:T(1024)} %copy-done.71), kind=kCustom, calls=%fused_computation.3 | custom fusion | bytes 2490444 | tf_op jit(solution)/shard_map/gather | solution.py:151
  92.1 1.4 pad_maximum_fusion.23
  93.5 1.3 pad_maximum_fusion.25
  96.2 0.8 fusion.69
  97.7 6.3 %stack.178 = f32[19,16384]{1,0:T(8,128)} concatenate(f32[1,16384]{1,0:T(1,128)} %bitcast.277, f32[1,16384]{1,0:T(1,128)} %bitcast.273, f32[1,16384]{1,0:T(1,128)} %bitcast.274, f32[1,16384]{1,0:T(1,128)} %bitcast.278, f32[1,16384]{1,0:T(1,128)} %bitcast.280, f32[1,16384]{1,0:T(1,128)S(1)} %bitcast.265, f32[1,16384]{1,0:T(1,128)S(1)} %bitcast.266, f32[1,16384]{1,0:T(1,128)} %bitcast.279, ...), dimensions={0} | concatenate | bytes 2490368 | tf_op jit(solution)/shard_map/stack | solution.py:173
  104.1 3.5 %fusion.4 = f32[19,16384]{1,0:T(8,128)S(1)} fusion(f32[19,19]{1,0:T(8,128)S(1)} %copy-done.59, f32[19,16384]{1,0:T(8,128)} %stack.178, f32[16384]{0:T(1024)S(1)} %bitcast.275, f32[16384]{0:T(1024)S(1)} %get-tuple-element.90, f32[19]{0:T(128)S(1)} %copy-done.70, f32[16384]{0:T(1024)S(1)} %get-tuple-element.93, f32[19]{0:T(128)S(1)} %copy-done.67, ...), kind=kOutput, calls=%fused_computation.13 | convolution fusion | flops 75333632 | bytes 2819796 | tf_op jit(solution)/shard_map/dot_general | solution.py:148
  107.9 1.0 copy-done.6
  109.2 1.3 fusion.23
  110.5 1.5 fusion.83
  112.0 2.2 %copy.59 = f32[19,16,8,1]{0,2,3,1:T(8,128)S(1)} copy(f32[19,16,8,1]{3,2,1,0:T(8,128)} %get-tuple-element.79) | data formatting | bytes 19456 | tf_op jit(solution)/shard_map/slice | solution.py:71
  114.2 1.5 collective-permute-start.5
  115.7 1.0 copy.57
  118.0 8.4 %all-gather = f32[8,16,8]{1,2,0:T(8,128)S(1)} all-gather(f32[2,16,8]{1,2,0:T(8,128)S(1)} %copy.63), channel_id=2, replica_groups=mesh['gx'=4,'gz'=8] {'gx'}, dimensions={0}, use_global_device_ids=true | all-gather | bytes 5120 | tf_op jit(solution)/shard_map/all_gather | solution.py:223
  127.0 1.3 copy.60
  128.3 2.2 %copy.58 = f32[19,16,8,1]{3,2,1,0:T(8,128)} copy(f32[19,16,8,1]{0,2,3,1:T(8,128)S(1)} %collective-permute-done.4) | data formatting | bytes 19456 | tf_op jit(solution)/shard_map/ppermute | solution.py:72
  130.6 1.6 pad_maximum_fusion.12
  132.2 0.8 fusion.46
  133.0 2.0 %pad_maximum_fusion = (f32[19,16,1,130]{3,2,1,0:T(1,128)S(1)}, f32[19,16,1,130]{3,2,1,0:T(1,128)S(1)}) fusion(f32[19,16,8,1]{3,2,1,0:T(8,128)S(1)} %copy.60, f32[19,16,8,128]{3,2,1,0:T(8,128)S(1)} %get-tuple-element.72, f32[19,16,8,1]{3,2,1,0:T(8,128)S(1)} %copy-done), kind=kLoop, calls=%fused_computation.56 | loop fusion | flops 158080 | bytes 1580800 | tf_op jit(solution)/shard_map/concatenate | solution.py:74
  136.2 2.4 %copy.115 = f32[19,16,8,128]{3,2,1,0:T(8,128)} copy(f32[19,16,8,128]{3,2,1,0:T(8,128)} %constant_dynamic-update-slice_fusion.69) | data formatting | bytes 2490368
  138.7 3.5 %collective-permute-start.7 = (f32[19,16,1,130]{3,2,1,0:T(1,128)S(1)}, f32[19,16,1,130]{3,2,1,0:T(1,128)S(1)}, u32[]{:S(2)}, u32[]{:S(2)}) collective-permute-start(f32[19,16,1,130]{3,2,1,0:T(1,128)S(1)} %get-tuple-element.58), channel_id=1, source_target_pairs={{1,0},{2,1},{3,2},{4,3},{5,4},{6,5},{7,6},{0,7},{9,8},{10,9},{11,1... | collective-permute-start | bytes 474248 | tf_op jit(solution)/shard_map/ppermute | solution.py:73
  142.9 5.4 %collective-permute-done.6 = f32[19,16,1,130]{3,2,1,0:T(1,128)S(1)} collective-permute-done((f32[19,16,1,130]{3,2,1,0:T(1,128)S(1)}, f32[19,16,1,130]{3,2,1,0:T(1,128)S(1)}, u32[]{:S(2)}, u32[]{:S(2)}) %collective-permute-start.6) | collective-permute-done | bytes 158112 | tf_op jit(solution)/shard_map/ppermute | solution.py:72
  153.3 0.7 constant_dynamic-update-slice_fusion.41
  154.7 0.8 constant_dynamic-update-slice_fusion.39
  156.2 0.8 constant_dynamic-update-slice_fusion.37
  157.7 1.9 %gather_fusion.5 = f32[5,8,128]{2,1,0:T(8,128)S(1)} fusion(f32[19,16,8,128]{3,2,1,0:T(8,128)} %constant_dynamic-update-slice_fusion.36, s32[5]{0:T(128)S(1)} %copy-done.48), kind=kCustom, calls=%fused_computation.5 | custom fusion | bytes 41000 | tf_op jit(solution)/shard_map/gather | solution.py:218
  159.6 2.5 %gather_fusion.4 = f32[5,8,128]{2,1,0:T(8,128)} fusion(f32[19,16,8,128]{3,2,1,0:T(8,128)} %constant_dynamic-update-slice_fusion.36, s32[5]{0:T(128)S(1)} %copy-done.47), kind=kCustom, calls=%fused_computation.4 | custom fusion | bytes 41000 | tf_op jit(solution)/shard_map/gather | solution.py:218
  162.1 0.8 pad_maximum_fusion.49
  162.9 9.1 %all_gather.13 = f32[2,5,8,512]{3,2,1,0:T(8,128)S(1)} all-gather(f32[2,5,8,128]{3,2,1,0:T(8,128)S(1)} %pad_maximum_fusion.49), channel_id=1, replica_groups=mesh['gx'=4,'gz'=8] {'gx'}, dimensions={3}, use_global_device_ids=true | all-gather | bytes 204800 | tf_op jit(solution)/shard_map/all_gather | solution.py:194
  (254 shorter events, 37.7 us)
Async XLA Ops:
  0.6 3.4 %copy-start.60 = (f32[19]{0:T(128)S(1)}, f32[19]{0:T(128)}, u32[]{:S(2)}) copy-start(f32[19]{0:T(128)} %constant.136) | copy-start | bytes 232
  0.6 3.4 %copy-start.63 = (f32[19]{0:T(128)S(1)}, f32[19]{0:T(128)}, u32[]{:S(2)}) copy-start(f32[19]{0:T(128)} %constant.134) | copy-start | bytes 232
  0.7 3.4 %copy-start.65 = (f32[19]{0:T(128)S(1)}, f32[19]{0:T(128)}, u32[]{:S(2)}) copy-start(f32[19]{0:T(128)} %constant.137) | copy-start | bytes 232
  0.7 3.4 %copy-start.68 = (f32[19]{0:T(128)S(1)}, f32[19]{0:T(128)}, u32[]{:S(2)}) copy-start(f32[19]{0:T(128)} %constant.138) | copy-start | bytes 232
  0.7 3.3 %copy-start.7 = (f32[19,16,8,128]{3,2,1,0:T(8,128)S(1)}, f32[19,16,8,128]{3,2,1,0:T(8,128)}, u32[]{:S(2)}) copy-start(f32[19,16,8,128]{3,2,1,0:T(8,128)} %param.36) | copy-start | bytes 3735556
  1.5 11.6 %copy-start.71 = (s32[1024]{0:T(1024)}, s32[1024]{0:T(1024)S(1)}, u32[]{:S(2)}) copy-start(s32[1024]{0:T(1024)S(1)} %pad_clamp_fusion) | copy-start | bytes 12292
  9.6 3.5 %copy-start.10 = (f32[19,16,8,128]{3,2,1,0:T(8,128)S(1)}, f32[19,16,8,128]{3,2,1,0:T(8,128)}, u32[]{:S(2)}) copy-start(f32[19,16,8,128]{3,2,1,0:T(8,128)} %get-tuple-element.71) | copy-start | bytes 3735556
  18.1 8.4 %copy-start.75 = (s32[2]{0:T(128)S(1)}, s32[2]{0:T(128)}, u32[]{:S(2)}) copy-start(s32[2]{0:T(128)} %param.38) | copy-start | bytes 28
  18.1 9.0 %copy-start.76 = (s32[2]{0:T(128)S(1)}, s32[2]{0:T(128)}, u32[]{:S(2)}) copy-start(s32[2]{0:T(128)} %param.39) | copy-start | bytes 28
  20.3 16.4 %collective-permute-start = (f32[19,16,8,1]{0,2,3,1:T(8,128)S(1)}, f32[19,16,8,1]{0,2,3,1:T(8,128)S(1)}, u32[]{:S(2)}, u32[]{:S(2)}) collective-permute-start(f32[19,16,8,1]{0,2,3,1:T(8,128)S(1)} %copy.51), channel_id=1, source_target_pairs={{0,8},{8,16},{16,24},{24,0},{1,9},{9,17},{17,25},{25,1},{2,10},{10... | collective-permute-start | bytes 29192 | tf_op jit(solution)/shard_map/ppermute | solution.py:72
  24.9 13.1 %collective-permute-start.1 = (f32[19,16,8,1]{0,2,3,1:T(8,128)}, f32[19,16,8,1]{0,2,3,1:T(8,128)}, u32[]{:S(2)}, u32[]{:S(2)}) collective-permute-start(f32[19,16,8,1]{0,2,3,1:T(8,128)} %copy.53), channel_id=1, source_target_pairs={{8,0},{16,8},{24,16},{0,24},{9,1},{17,9},{25,17},{1,25},{10,2},{18... | collective-permute-start | bytes 29192 | tf_op jit(solution)/shard_map/ppermute | solution.py:73
  41.1 1.8 copy-start.2
  48.8 8.9 %collective-permute-start.2 = (f32[19,16,1,130]{3,2,1,0:T(1,128)S(1)}, f32[19,16,1,130]{3,2,1,0:T(1,128)S(1)}, u32[]{:S(2)}, u32[]{:S(2)}) collective-permute-start(f32[19,16,1,130]{3,2,1,0:T(1,128)S(1)} %get-tuple-element.63), channel_id=1, source_target_pairs={{0,1},{1,2},{2,3},{3,4},{4,5},{5,6},{6,7},{7,0},{8,9},{9,10},{10,1... | collective-permute-start | bytes 474248 | tf_op jit(solution)/shard_map/ppermute | solution.py:72
  48.8 9.6 %collective-permute-start.3 = (f32[19,16,1,130]{3,2,1,0:T(1,128)S(1)}, f32[19,16,1,130]{3,2,1,0:T(1,128)S(1)}, u32[]{:S(2)}, u32[]{:S(2)}) collective-permute-start(f32[19,16,1,130]{3,2,1,0:T(1,128)S(1)} %get-tuple-element.62), channel_id=1, source_target_pairs={{1,0},{2,1},{3,2},{4,3},{5,4},{6,5},{7,6},{0,7},{9,8},{10,9},{11,1... | collective-permute-start | bytes 474248 | tf_op jit(solution)/shard_map/ppermute | solution.py:73
  66.6 2.6 %copy-start.47 = (s32[5]{0:T(128)S(1)}, s32[5]{0:T(128)}, u32[]{:S(2)}) copy-start(s32[5]{0:T(128)} %constant.208) | copy-start | bytes 64
  67.3 17.1 %copy-start.72 = (f32[5]{0:T(128)S(1)}, f32[5]{0:T(128)}, u32[]{:S(2)}) copy-start(f32[5]{0:T(128)} %constant.144) | copy-start | bytes 64
  71.7 12.9 %copy-start.17 = (f32[15,8,128]{2,1,0:T(8,128)S(1)}, f32[15,8,128]{2,1,0:T(8,128)}, u32[]{:S(2)}) copy-start(f32[15,8,128]{2,1,0:T(8,128)} %get-tuple-element.85) | copy-start | bytes 184324
  71.7 13.5 %copy-start.3 = (f32[19,16,8,1]{3,2,1,0:T(8,128)S(1)}, f32[19,16,8,1]{3,2,1,0:T(8,128)}, u32[]{:S(2)}) copy-start(f32[19,16,8,1]{3,2,1,0:T(8,128)} %copy.54) | copy-start | bytes 29188
  84.6 2.2 %copy-start.53 = (f32[1,8,128]{2,1,0:T(8,128)}, f32[1,8,128]{2,1,0:T(8,128)S(1)}, u32[]{:S(2)}) copy-start(f32[1,8,128]{2,1,0:T(8,128)S(1)} %get-tuple-element.111) | copy-start | bytes 12292
  84.6 2.2 %copy-start.51 = (f32[1,8,128]{2,1,0:T(8,128)}, f32[1,8,128]{2,1,0:T(8,128)S(1)}, u32[]{:S(2)}) copy-start(f32[1,8,128]{2,1,0:T(8,128)S(1)} %get-tuple-element.110) | copy-start | bytes 12292
  84.6 2.3 %copy-start.49 = (f32[1,8,128]{2,1,0:T(8,128)}, f32[1,8,128]{2,1,0:T(8,128)S(1)}, u32[]{:S(2)}) copy-start(f32[1,8,128]{2,1,0:T(8,128)S(1)} %get-tuple-element.109) | copy-start | bytes 12292
  85.5 2.5 %copy-start.61 = (f32[19]{0:T(128)S(1)}, f32[19]{0:T(128)}, u32[]{:S(2)}) copy-start(f32[19]{0:T(128)} %constant.136) | copy-start | bytes 232
  85.5 2.5 %copy-start.66 = (f32[19]{0:T(128)S(1)}, f32[19]{0:T(128)}, u32[]{:S(2)}) copy-start(f32[19]{0:T(128)} %constant.137) | copy-start | bytes 232
  85.5 2.5 %copy-start.69 = (f32[19]{0:T(128)S(1)}, f32[19]{0:T(128)}, u32[]{:S(2)}) copy-start(f32[19]{0:T(128)} %constant.138) | copy-start | bytes 232
  89.0 2.3 %copy-start.16 = (f32[15,8,128]{2,1,0:T(8,128)S(1)}, f32[15,8,128]{2,1,0:T(8,128)}, u32[]{:S(2)}) copy-start(f32[15,8,128]{2,1,0:T(8,128)} %get-tuple-element.84) | copy-start | bytes 184324
  89.0 2.3 %copy-start.18 = (f32[15,8,128]{2,1,0:T(8,128)S(1)}, f32[15,8,128]{2,1,0:T(8,128)}, u32[]{:S(2)}) copy-start(f32[15,8,128]{2,1,0:T(8,128)} %get-tuple-element.85) | copy-start | bytes 184324
  89.0 3.0 %copy-start.28 = (f32[15,8,128]{2,1,0:T(8,128)S(1)}, f32[15,8,128]{2,1,0:T(8,128)}, u32[]{:S(2)}) copy-start(f32[15,8,128]{2,1,0:T(8,128)} %copy-done.27) | copy-start | bytes 184324
  89.1 3.0 %copy-start.30 = (f32[15,8,128]{2,1,0:T(8,128)S(1)}, f32[15,8,128]{2,1,0:T(8,128)}, u32[]{:S(2)}) copy-start(f32[15,8,128]{2,1,0:T(8,128)} %copy-done.29) | copy-start | bytes 184324
  89.1 3.0 %copy-start.52 = (f32[1,8,128]{2,1,0:T(8,128)S(1)}, f32[1,8,128]{2,1,0:T(8,128)}, u32[]{:S(2)}) copy-start(f32[1,8,128]{2,1,0:T(8,128)} %copy-done.51) | copy-start | bytes 12292
  89.1 4.4 %copy-start.12 = (f32[15,8,128]{2,1,0:T(8,128)S(1)}, f32[15,8,128]{2,1,0:T(8,128)}, u32[]{:S(2)}) copy-start(f32[15,8,128]{2,1,0:T(8,128)} %get-tuple-element.68) | copy-start | bytes 184324
  89.1 4.4 %copy-start.14 = (f32[15,8,128]{2,1,0:T(8,128)S(1)}, f32[15,8,128]{2,1,0:T(8,128)}, u32[]{:S(2)}) copy-start(f32[15,8,128]{2,1,0:T(8,128)} %get-tuple-element.69) | copy-start | bytes 184324
  89.1 5.7 %copy-start.22 = (f32[15,8,128]{2,1,0:T(8,128)S(1)}, f32[15,8,128]{2,1,0:T(8,128)}, u32[]{:S(2)}) copy-start(f32[15,8,128]{2,1,0:T(8,128)} %copy-done.21) | copy-start | bytes 184324
  89.1 5.7 %copy-start.26 = (f32[15,8,128]{2,1,0:T(8,128)S(1)}, f32[15,8,128]{2,1,0:T(8,128)}, u32[]{:S(2)}) copy-start(f32[15,8,128]{2,1,0:T(8,128)} %copy-done.25) | copy-start | bytes 184324
  89.1 6.4 %copy-start.20 = (f32[15,8,128]{2,1,0:T(8,128)S(1)}, f32[15,8,128]{2,1,0:T(8,128)}, u32[]{:S(2)}) copy-start(f32[15,8,128]{2,1,0:T(8,128)} %copy-done.19) | copy-start | bytes 184324
  89.1 6.4 %copy-start.24 = (f32[15,8,128]{2,1,0:T(8,128)S(1)}, f32[15,8,128]{2,1,0:T(8,128)}, u32[]{:S(2)}) copy-start(f32[15,8,128]{2,1,0:T(8,128)} %copy-done.23) | copy-start | bytes 184324
  89.1 6.4 %copy-start.50 = (f32[1,8,128]{2,1,0:T(8,128)S(1)}, f32[1,8,128]{2,1,0:T(8,128)}, u32[]{:S(2)}) copy-start(f32[1,8,128]{2,1,0:T(8,128)} %copy-done.49) | copy-start | bytes 12292
  91.3 4.8 %copy-start.35 = (f32[16,8,128]{2,1,0:T(8,128)S(1)}, f32[16,8,128]{2,1,0:T(8,128)}, u32[]{:S(2)}) copy-start(f32[16,8,128]{2,1,0:T(8,128)} %get-tuple-element.9) | copy-start | bytes 196612
  91.3 4.8 %copy-start.38 = (f32[1,16,8,128]{3,2,1,0:T(8,128)S(1)}, f32[1,16,8,128]{3,2,1,0:T(8,128)}, u32[]{:S(2)}) copy-start(f32[1,16,8,128]{3,2,1,0:T(8,128)} %get-tuple-element.43) | copy-start | bytes 196612
  91.3 4.8 %copy-start.39 = (f32[1,16,8,128]{3,2,1,0:T(8,128)S(1)}, f32[1,16,8,128]{3,2,1,0:T(8,128)}, u32[]{:S(2)}) copy-start(f32[1,16,8,128]{3,2,1,0:T(8,128)} %get-tuple-element.41) | copy-start | bytes 196612
  91.4 4.8 %copy-start.54 = (f32[1,8,128]{2,1,0:T(8,128)S(1)}, f32[1,8,128]{2,1,0:T(8,128)}, u32[]{:S(2)}) copy-start(f32[1,8,128]{2,1,0:T(8,128)} %copy-done.53) | copy-start | bytes 12292
  91.4 4.8 %copy-start.56 = (f32[1,8,128]{2,1,0:T(8,128)S(1)}, f32[1,8,128]{2,1,0:T(8,128)}, u32[]{:S(2)}) copy-start(f32[1,8,128]{2,1,0:T(8,128)} %copy-done.55) | copy-start | bytes 12292
  92.0 5.5 %copy-start.33 = (f32[1,16,8,128]{3,2,1,0:T(8,128)S(1)}, f32[1,16,8,128]{3,2,1,0:T(8,128)}, u32[]{:S(2)}) copy-start(f32[1,16,8,128]{3,2,1,0:T(8,128)} %sub.117) | copy-start | bytes 196612
  92.1 5.5 %copy-start.37 = (f32[16,8,128]{2,1,0:T(8,128)S(1)}, f32[16,8,128]{2,1,0:T(8,128)}, u32[]{:S(2)}) copy-start(f32[16,8,128]{2,1,0:T(8,128)} %copy-done.36) | copy-start | bytes 196612
  92.1 5.5 %copy-start.41 = (f32[16,8,128]{2,1,0:T(8,128)S(1)}, f32[16,8,128]{2,1,0:T(8,128)}, u32[]{:S(2)}) copy-start(f32[16,8,128]{2,1,0:T(8,128)} %get-tuple-element.7) | copy-start | bytes 196612
  92.1 5.5 %copy-start.42 = (f32[16,8,128]{2,1,0:T(8,128)S(1)}, f32[16,8,128]{2,1,0:T(8,128)}, u32[]{:S(2)}) copy-start(f32[16,8,128]{2,1,0:T(8,128)} %get-tuple-element.8) | copy-start | bytes 196612
  97.6 6.4 %copy-start.32 = (f32[1,16,8,128]{3,2,1,0:T(8,128)S(1)}, f32[1,16,8,128]{3,2,1,0:T(8,128)}, u32[]{:S(2)}) copy-start(f32[1,16,8,128]{3,2,1,0:T(8,128)} %copy-done.31) | copy-start | bytes 196612
  97.6 6.4 %copy-start.59 = (f32[19,19]{1,0:T(8,128)S(1)}, f32[19,19]{1,0:T(8,128)}, u32[]{:S(2)}) copy-start(f32[19,19]{1,0:T(8,128)} %constant.119.clone) | copy-start | bytes 4336
  97.6 6.4 %copy-start.62 = (f32[19]{0:T(128)S(1)}, f32[19]{0:T(128)}, u32[]{:S(2)}) copy-start(f32[19]{0:T(128)} %constant.136) | copy-start | bytes 232
  97.6 6.4 %copy-start.64 = (f32[19]{0:T(128)S(1)}, f32[19]{0:T(128)}, u32[]{:S(2)}) copy-start(f32[19]{0:T(128)} %constant.134) | copy-start | bytes 232
  97.7 6.4 %copy-start.67 = (f32[19]{0:T(128)S(1)}, f32[19]{0:T(128)}, u32[]{:S(2)}) copy-start(f32[19]{0:T(128)} %constant.137) | copy-start | bytes 232
  97.7 6.4 %copy-start.70 = (f32[19]{0:T(128)S(1)}, f32[19]{0:T(128)}, u32[]{:S(2)}) copy-start(f32[19]{0:T(128)} %constant.138) | copy-start | bytes 232
  107.6 1.7 copy-start.9
  112.0 5.2 %copy-start.34 = (f32[1,16,8,128]{3,2,1,0:T(8,128)S(1)}, f32[1,16,8,128]{3,2,1,0:T(8,128)}, u32[]{:S(2)}) copy-start(f32[1,16,8,128]{3,2,1,0:T(8,128)} %sub.117) | copy-start | bytes 196612
  114.2 12.8 %collective-permute-start.5 = (f32[19,16,8,1]{0,2,3,1:T(8,128)S(1)}, f32[19,16,8,1]{0,2,3,1:T(8,128)S(1)}, u32[]{:S(2)}, u32[]{:S(2)}) collective-permute-start(f32[19,16,8,1]{0,2,3,1:T(8,128)S(1)} %copy.59), channel_id=1, source_target_pairs={{8,0},{16,8},{24,16},{0,24},{9,1},{17,9},{25,17},{1,25},{10,2},{18... | collective-permute-start | bytes 29192 | tf_op jit(solution)/shard_map/ppermute | solution.py:73
  116.7 11.7 %collective-permute-start.4 = (f32[19,16,8,1]{0,2,3,1:T(8,128)S(1)}, f32[19,16,8,1]{0,2,3,1:T(8,128)S(1)}, u32[]{:S(2)}, u32[]{:S(2)}) collective-permute-start(f32[19,16,8,1]{0,2,3,1:T(8,128)S(1)} %copy.57), channel_id=1, source_target_pairs={{0,8},{8,16},{16,24},{24,0},{1,9},{9,17},{17,25},{25,1},{2,10},{10... | collective-permute-start | bytes 29192 | tf_op jit(solution)/shard_map/ppermute | solution.py:72
  138.7 9.6 %collective-permute-start.6 = (f32[19,16,1,130]{3,2,1,0:T(1,128)S(1)}, f32[19,16,1,130]{3,2,1,0:T(1,128)S(1)}, u32[]{:S(2)}, u32[]{:S(2)}) collective-permute-start(f32[19,16,1,130]{3,2,1,0:T(1,128)S(1)} %get-tuple-element.59), channel_id=1, source_target_pairs={{0,1},{1,2},{2,3},{3,4},{4,5},{5,6},{6,7},{7,0},{8,9},{9,10},{10,1... | collective-permute-start | bytes 474248 | tf_op jit(solution)/shard_map/ppermute | solution.py:72
  138.7 10.3 %collective-permute-start.7 = (f32[19,16,1,130]{3,2,1,0:T(1,128)S(1)}, f32[19,16,1,130]{3,2,1,0:T(1,128)S(1)}, u32[]{:S(2)}, u32[]{:S(2)}) collective-permute-start(f32[19,16,1,130]{3,2,1,0:T(1,128)S(1)} %get-tuple-element.58), channel_id=1, source_target_pairs={{1,0},{2,1},{3,2},{4,3},{5,4},{6,5},{7,6},{0,7},{9,8},{10,9},{11,1... | collective-permute-start | bytes 474248 | tf_op jit(solution)/shard_map/ppermute | solution.py:73
  157.0 15.2 %copy-start.74 = (f32[5]{0:T(128)S(1)}, f32[5]{0:T(128)}, u32[]{:S(2)}) copy-start(f32[5]{0:T(128)} %constant.146) | copy-start | bytes 64
  157.7 14.7 %copy-start.73 = (f32[5]{0:T(128)S(1)}, f32[5]{0:T(128)}, u32[]{:S(2)}) copy-start(f32[5]{0:T(128)} %constant.144) | copy-start | bytes 64
  162.1 10.4 %copy-start.46 = (f32[15,8,128]{2,1,0:T(8,128)S(1)}, f32[15,8,128]{2,1,0:T(8,128)}, u32[]{:S(2)}) copy-start(f32[15,8,128]{2,1,0:T(8,128)} %get-tuple-element.75) | copy-start | bytes 184324
  162.1 11.1 %copy-start.1 = (f32[19,16,8,1]{3,2,1,0:T(8,128)S(1)}, f32[19,16,8,1]{3,2,1,0:T(8,128)}, u32[]{:S(2)}) copy-start(f32[19,16,8,1]{3,2,1,0:T(8,128)} %copy.58) | copy-start | bytes 29188
  173.2 2.1 %copy-start.45 = (f32[15,8,128]{2,1,0:T(8,128)S(1)}, f32[15,8,128]{2,1,0:T(8,128)}, u32[]{:S(2)}) copy-start(f32[15,8,128]{2,1,0:T(8,128)} %get-tuple-element.74) | copy-start | bytes 184324
  173.2 2.8 %copy-start.44 = (f32[15,8,128]{2,1,0:T(8,128)S(1)}, f32[15,8,128]{2,1,0:T(8,128)}, u32[]{:S(2)}) copy-start(f32[15,8,128]{2,1,0:T(8,128)} %get-tuple-element.66) | copy-start | bytes 184324
  173.2 4.0 %copy-start.43 = (f32[15,8,128]{2,1,0:T(8,128)S(1)}, f32[15,8,128]{2,1,0:T(8,128)}, u32[]{:S(2)}) copy-start(f32[15,8,128]{2,1,0:T(8,128)} %get-tuple-element.65) | copy-start | bytes 184324
  (22 other events, 28.3 us)
